TPU v7x, 32 devices: a whole 2x2x4 slice. The times are simulated.
32 devices in a mesh: tm: 4 (over y, core), space: 8 (over z, x).
Axes of the slice: x: 2, y: 2, z: 4, core: 2. Of those that a mesh axis runs over, the one named last changes fastest.
Arguments:
- base: float32 [2, 4, 16, 64, 128], P(None, 'tm', 'space'), may hold values from -6 to 6
- phi_prev: float32 [4, 16, 64, 128], P('tm', 'space'), may hold values from -6 to 6
- masks: int32 [2, 16, 64, 128], P(None, 'space'), may hold values from 0 to 1, as said below
- enc_w: bfloat16 [16, 1, 3, 3, 3], replicated, may hold values from -1.25 to 1.25
- enc_b: float32 [16], replicated, may hold values from -0.5 to 0.5
- in_w: bfloat16 [2, 16, 1, 3, 3, 3], replicated, may hold values from -1.25 to 1.25
- ctx_w: bfloat16 [2, 16, 16], replicated, may hold values from -1.5 to 1.5
- hid_b: float32 [2, 16], replicated, may hold values from -0.5 to 0.5
- mid_w: bfloat16 [2, 16, 16, 3, 3, 3], replicated, may hold values from -0.3125 to 0.3125
- mid_b: float32 [2, 16], replicated, may hold values from -0.5 to 0.5
- out_w: bfloat16 [2, 2, 16], replicated, may hold values from -1.5 to 1.5
- out_b: float32 [2, 2], replicated, may hold values from -0.5 to 0.5
Outputs:
- samples: float32 [2, 4, 16, 64, 128], P(None, 'tm', 'space')
- logdet: float32 [2, 4], P(None, 'tm')
Inputs may be any that keep to these rules, and one draw needn't show every extreme that they name: `masks`: each layer's mask is a checkerboard of 0 and 1 in the three lattice coordinates, its parity chosen per layer.
All inputs are finite; a program needn't handle non-finite values.
Results may differ from a plain program's by a relative error of at most 0.0043.
Values may be sent and summed in bfloat16 or wider, within the bound.
No kernel may reach another device: no remote copies, remote signals or barrier semaphores. Data moves between devices by JAX's collectives and lax.ppermute only.
A program may use at most 128 MiB of HBM per device.

v0:
```python
import jax
import jax.numpy as jnp
from jax import lax
from jax.sharding import PartitionSpec as P

LAYERS = 2
TICKS = 2


def with_halo(block, sides, width):
    for axis, dim in sides:
        count = lax.axis_size(axis)
        forward = [(i, i + 1) for i in range(count - 1)]
        forward.append((count - 1, 0))
        backward = [(target, source) for source, target in forward]
        low = lax.ppermute(
            lax.slice_in_dim(block, block.shape[dim] - width, None, axis=dim), axis, forward
        )
        high = lax.ppermute(lax.slice_in_dim(block, 0, width, axis=dim), axis, backward)
        block = jnp.concatenate([low, block, high], axis=dim)
    return block


def passed_along(value, axis, steps):
    count = lax.axis_size(axis)
    pairs = [(source, (source + steps) % count) for source in range(count)]
    return lax.ppermute(value, axis, pairs)


def conv_slab(padded, kernel):
    widened = jnp.pad(padded, ((0, 0), (0, 0), (1, 1), (1, 1)), mode="wrap")
    return lax.conv_general_dilated(
        widened[None],
        kernel,
        (1, 1, 1),
        "VALID",
        dimension_numbers=("NCDHW", "OIDHW", "NCDHW"),
        preferred_element_type=jnp.float32,
    )[0]


def encode(slice_field, depth, enc_w, enc_b):
    padded = with_halo(slice_field[None], (("space", 1),), depth)
    value = conv_slab(padded, enc_w) + enc_b[:, None, None, None]
    return jnp.tanh(value).astype(jnp.bfloat16)


def context_of(phi, depth, enc_w, enc_b):
    rounded = phi.astype(jnp.bfloat16)
    features = encode(rounded, depth, enc_w, enc_b)
    return passed_along(features, "tm", 1)


def shards(base, phi_prev, masks, enc_w, enc_b, in_w, ctx_w, hid_b, mid_w, mid_b, out_w, out_b):
    sites_total = masks.shape[1] * masks.shape[2] * masks.shape[3] * lax.axis_size("space")
    depth = 1
    previous = phi_prev[0]
    samples = []
    logdets = []
    for tick in range(TICKS):
        context = context_of(previous, depth, enc_w, enc_b)
        phi = base[tick, 0]
        total = jnp.zeros((), jnp.float32)
        for layer in range(LAYERS):
            keep = masks[layer].astype(jnp.float32)
            frozen = (keep * phi).astype(jnp.bfloat16)[None]
            frozen_rim = with_halo(frozen, (("space", 1),), depth)
            mixed = jnp.einsum(
                "oc,cxyz->oxyz", ctx_w[layer], context, preferred_element_type=jnp.float32
            )
            first = conv_slab(frozen_rim, in_w[layer]) + mixed + hid_b[layer][:, None, None, None]
            hidden = jnp.tanh(first).astype(jnp.bfloat16)
            hidden_wide = with_halo(hidden, (("space", 1),), 1)
            second = conv_slab(hidden_wide, mid_w[layer]) + mid_b[layer][:, None, None, None]
            deeper = jnp.tanh(second).astype(jnp.bfloat16)
            output = (
                jnp.einsum(
                    "oc,cxyz->oxyz", out_w[layer], deeper, preferred_element_type=jnp.float32
                )
                + out_b[layer][:, None, None, None]
            )
            scale = jnp.tanh(output[0])
            phi = keep * phi + (1.0 - keep) * (phi * jnp.exp(scale) + output[1])
            total = total + jnp.sum((1.0 - keep) * scale)
        whole = lax.psum(total, "space")
        samples.append(phi)
        logdets.append(whole / sites_total)
        previous = phi
    return (jnp.stack(samples)[:, None], jnp.stack(logdets)[:, None])


def solution(mesh):
    in_specs = (
        P(None, "tm", "space", None, None),
        P("tm", "space", None, None),
        P(None, "space", None, None),
        P(),
        P(),
        P(),
        P(),
        P(),
        P(),
        P(),
        P(),
        P(),
    )
    out_specs = (P(None, "tm", "space", None, None), P(None, "tm"))
    return jax.shard_map(shards, mesh=mesh, in_specs=in_specs, out_specs=out_specs, check_vma=False)
```

profile of v0, /device:TPU:0, one launch (start us, length us, event | category | flops | bytes accessed | tf_op | source)
XLA Modules:
  0.0 497.4 jit_solution(10493341801283417893)
XLA Ops:
  17.9 16.2 %fusion.116 = f32[2,64,8,17,16]{4,2,3,1,0:T(8,128)} fusion(bf16[1,4,66,8,19]{3,0,4,2,1:T(2,128)(2,1)S(1)} %copy.257, bf16[16,1,3,3,3]{0,4,3,2,1:T(4,128)(2,1)S(1)} %copy-done), kind=kOutput, calls=%fused_computation.187 | convolution fusion | flops 15040512 | bytes 1195232 | tf_op jit(solution)/shard_map/conv_general_dilated | solution.py:32
  34.1 5.6 %copy.259 = f32[2,64,8,17,16]{1,4,3,2,0:T(8,128)S(1)} copy(f32[2,64,8,17,16]{4,2,3,1,0:T(8,128)} %fusion.116) | data formatting | bytes 2228224 | tf_op jit(solution)/shard_map/conv_general_dilated | solution.py:32
  45.6 17.2 %fusion.112 = f32[2,64,8,17,16]{4,2,3,1,0:T(8,128)} fusion(bf16[1,4,66,8,19]{3,0,4,2,1:T(2,128)(2,1)} %copy.251, bf16[2,16,1,3,3,3]{1,0,5,4,3,2:T(2,128)(2,1)S(1)} %copy-done.41), kind=kOutput, calls=%fused_computation.183 | convolution fusion | flops 15040512 | bytes 1196096 | tf_op jit(solution)/shard_map/conv_general_dilated | solution.py:32
  62.8 6.6 %copy.253 = f32[2,64,8,17,16]{1,4,3,2,0:T(8,128)} copy(f32[2,64,8,17,16]{4,2,3,1,0:T(8,128)} %fusion.112) | data formatting | bytes 2228224 | tf_op jit(solution)/shard_map/conv_general_dilated | solution.py:32
  110.9 7.8 %copy.263 = bf16[16,4,66,1,8,17]{0,4,5,2,1,3:T(8,128)(2,1)} copy(bf16[16,4,66,1,8,17]{2,0,5,4,1,3:T(8,128)(2,1)S(1)} %bitcast.268) | data formatting | bytes 2297856 | tf_op jit(solution)/shard_map/conv_general_dilated | solution.py:32
  120.2 15.9 %fusion.6 = f32[2,64,8,17,16]{4,2,3,1,0:T(8,128)} fusion(bf16[16,4,66,1,7,2]{0,4,5,2,1,3:T(8,128)(2,1)S(1)} %slice.404, bf16[16,4,66,1,8,17]{0,4,5,2,1,3:T(8,128)(2,1)} %copy.263, bf16[2,16,16,3,3,3]{2,1,5,4,3,0:T(8,128)(2,1)S(1)} %copy-done.37), kind=kOutput, calls=%fused_computation.7 | convolution fusion | flops 244500480 | bytes 3454976 | tf_op jit(solution)/shard_map/conv_general_dilated | solution.py:32
  136.1 6.0 %copy.264 = f32[2,64,8,17,16]{1,4,3,2,0:T(8,128)S(1)} copy(f32[2,64,8,17,16]{4,2,3,1,0:T(8,128)} %fusion.6) | data formatting | bytes 2228224 | tf_op jit(solution)/shard_map/conv_general_dilated | solution.py:32
  160.3 16.2 %fusion.108 = f32[2,64,8,17,16]{4,2,3,1,0:T(8,128)} fusion(bf16[1,4,66,8,19]{3,0,4,2,1:T(2,128)(2,1)S(1)} %copy.270, bf16[2,16,1,3,3,3]{1,0,5,4,3,2:T(2,128)(2,1)S(1)} %copy-done.42), kind=kOutput, calls=%fused_computation.179 | convolution fusion | flops 15040512 | bytes 1196096 | tf_op jit(solution)/shard_map/conv_general_dilated | solution.py:32
  176.5 5.6 %copy.272 = f32[2,64,8,17,16]{1,4,3,2,0:T(8,128)S(1)} copy(f32[2,64,8,17,16]{4,2,3,1,0:T(8,128)} %fusion.108) | data formatting | bytes 2228224 | tf_op jit(solution)/shard_map/conv_general_dilated | solution.py:32
  191.5 6.3 %copy.283 = bf16[1,4,66,8,19]{3,0,4,2,1:T(2,128)(2,1)S(1)} copy(bf16[1,4,66,8,19]{2,1,4,3,0:T(4,128)(2,1)} %fusion.77) | data formatting | bytes 160512 | tf_op jit(solution)/shard_map/conv_general_dilated | solution.py:32
  197.7 16.9 %fusion.110 = f32[2,64,8,17,16]{4,2,3,1,0:T(8,128)} fusion(bf16[1,4,66,8,19]{3,0,4,2,1:T(2,128)(2,1)S(1)} %copy.283, bf16[2,16,1,3,3,3]{1,0,5,4,3,2:T(2,128)(2,1)} %param.17), kind=kOutput, calls=%fused_computation.181 | convolution fusion | flops 15040512 | bytes 1196096 | tf_op jit(solution)/shard_map/conv_general_dilated | solution.py:32
  226.9 5.9 %copy.344 = bf16[16,4,66,1,130]{2,0,4,1,3:T(8,128)(2,1)} copy(bf16[16,4,66,1,130]{4,0,2,1,3:T(8,128)(2,1)} %maximum_bitcast_fusion.1) | data formatting | bytes 2196480
  236.2 9.2 %copy.276 = bf16[16,4,66,1,8,17]{0,4,5,2,1,3:T(8,128)(2,1)} copy(bf16[16,4,66,1,8,17]{2,0,5,4,1,3:T(8,128)(2,1)} %bitcast.269) | data formatting | bytes 2297856 | tf_op jit(solution)/shard_map/conv_general_dilated | solution.py:32
  247.0 16.2 %fusion.10 = f32[2,64,8,17,16]{4,2,3,1,0:T(8,128)} fusion(bf16[16,4,66,1,7,2]{0,4,5,2,1,3:T(8,128)(2,1)S(1)} %slice.418, bf16[16,4,66,1,8,17]{0,4,5,2,1,3:T(8,128)(2,1)} %copy.276, bf16[2,16,16,3,3,3]{2,1,5,4,3,0:T(8,128)(2,1)S(1)} %copy-done.38), kind=kOutput, calls=%fused_computation.10 | convolution fusion | flops 244500480 | bytes 3454976 | tf_op jit(solution)/shard_map/conv_general_dilated | solution.py:32
  263.1 6.6 %copy.277 = f32[2,64,8,17,16]{1,4,3,2,0:T(8,128)} copy(f32[2,64,8,17,16]{4,2,3,1,0:T(8,128)} %fusion.10) | data formatting | bytes 2228224 | tf_op jit(solution)/shard_map/conv_general_dilated | solution.py:32
  287.7 16.2 %fusion.114 = f32[2,64,8,17,16]{4,2,3,1,0:T(8,128)} fusion(bf16[1,4,66,8,19]{3,0,4,2,1:T(2,128)(2,1)S(1)} %copy.290, bf16[16,1,3,3,3]{0,4,3,2,1:T(4,128)(2,1)S(1)} %copy-done), kind=kOutput, calls=%fused_computation.185 | convolution fusion | flops 15040512 | bytes 1195232 | tf_op jit(solution)/shard_map/conv_general_dilated | solution.py:32
  346.3 7.8 %copy.296 = bf16[16,4,66,1,8,17]{0,4,5,2,1,3:T(8,128)(2,1)} copy(bf16[16,4,66,1,8,17]{2,0,5,4,1,3:T(8,128)(2,1)S(1)} %bitcast.270) | data formatting | bytes 2297856 | tf_op jit(solution)/shard_map/conv_general_dilated | solution.py:32
  355.6 15.9 %fusion.14 = f32[2,64,8,17,16]{4,2,3,1,0:T(8,128)} fusion(bf16[16,4,66,1,7,2]{0,4,5,2,1,3:T(8,128)(2,1)S(1)} %slice.438, bf16[16,4,66,1,8,17]{0,4,5,2,1,3:T(8,128)(2,1)} %copy.296, bf16[2,16,16,3,3,3]{2,1,5,4,3,0:T(8,128)(2,1)S(1)} %copy-done.39), kind=kOutput, calls=%fused_computation.13 | convolution fusion | flops 244500480 | bytes 3454976 | tf_op jit(solution)/shard_map/conv_general_dilated | solution.py:32
  371.5 5.8 %copy.297 = f32[2,64,8,17,16]{1,4,3,2,0:T(8,128)S(1)} copy(f32[2,64,8,17,16]{4,2,3,1,0:T(8,128)} %fusion.14) | data formatting | bytes 2228224 | tf_op jit(solution)/shard_map/conv_general_dilated | solution.py:32
  391.2 16.2 %fusion.106 = f32[2,64,8,17,16]{4,2,3,1,0:T(8,128)} fusion(bf16[1,4,66,8,19]{3,0,4,2,1:T(2,128)(2,1)S(1)} %copy.303, bf16[2,16,1,3,3,3]{1,0,5,4,3,2:T(2,128)(2,1)S(1)} %copy-done.43), kind=kOutput, calls=%fused_computation.177 | convolution fusion | flops 15040512 | bytes 1196096 | tf_op jit(solution)/shard_map/conv_general_dilated | solution.py:32
  435.9 7.8 %copy.309 = bf16[16,4,66,1,8,17]{0,4,5,2,1,3:T(8,128)(2,1)} copy(bf16[16,4,66,1,8,17]{2,0,5,4,1,3:T(8,128)(2,1)S(1)} %bitcast.267) | data formatting | bytes 2297856 | tf_op jit(solution)/shard_map/conv_general_dilated | solution.py:32
  445.3 15.9 %fusion.18 = f32[2,64,8,17,16]{4,2,3,1,0:T(8,128)} fusion(bf16[16,4,66,1,7,2]{0,4,5,2,1,3:T(8,128)(2,1)S(1)} %slice.452, bf16[16,4,66,1,8,17]{0,4,5,2,1,3:T(8,128)(2,1)} %copy.309, bf16[2,16,16,3,3,3]{2,1,5,4,3,0:T(8,128)(2,1)S(1)} %copy-done.40), kind=kOutput, calls=%fused_computation.16 | convolution fusion | flops 244500480 | bytes 3454976 | tf_op jit(solution)/shard_map/conv_general_dilated | solution.py:32
  461.2 5.6 %copy.310 = f32[2,64,8,17,16]{1,4,3,2,0:T(8,128)S(1)} copy(f32[2,64,8,17,16]{4,2,3,1,0:T(8,128)} %fusion.18) | data formatting | bytes 2228224 | tf_op jit(solution)/shard_map/conv_general_dilated | solution.py:32
  472.4 22.0 %all-reduce = (f32[]{:T(128)}, f32[]{:T(128)}) all-reduce(f32[]{:T(128)S(6)} %add.232, f32[]{:T(128)S(6)} %add.231), channel_id=1, replica_groups=mesh['tm'=4,'space'=8] {'space'}, use_global_device_ids=true, to_apply=%region_5.6 | all-reduce | flops 2 | bytes 16 | tf_op jit(solution)/shard_map/psum | solution.py:85
  (283 shorter events, 219.7 us)
Async XLA Ops:
  1.5 11.8 %collective-permute-start.2 = (bf16[1,1,64,128]{3,2,1,0:T(8,128)(2,1)S(1)}, bf16[1,1,64,128]{3,2,1,0:T(8,128)(2,1)S(1)}, u32[]{:S(2)}, u32[]{:S(2)}) collective-permute-start(bf16[1,1,64,128]{3,2,1,0:T(8,128)(2,1)S(1)} %get-tuple-element.84), channel_id=1, source_target_pairs={{0,1},{1,2},{2,3},{3,4},{4,5},{5,6},{6,7},{7,0},{8,9},{9,10},{10,1... | collective-permute-start | bytes 49160 | tf_op jit(solution)/shard_map/ppermute | solution.py:16
  4.5 8.8 %collective-permute-start.3 = (bf16[1,1,64,128]{3,2,1,0:T(8,128)(2,1)S(1)}, bf16[1,1,64,128]{3,2,1,0:T(8,128)(2,1)S(1)}, u32[]{:S(2)}, u32[]{:S(2)}) collective-permute-start(bf16[1,1,64,128]{3,2,1,0:T(8,128)(2,1)S(1)} %get-tuple-element.85), channel_id=1, source_target_pairs={{1,0},{2,1},{3,2},{4,3},{5,4},{6,5},{7,6},{0,7},{9,8},{10,9},{11,1... | collective-permute-start | bytes 49160 | tf_op jit(solution)/shard_map/ppermute | solution.py:19
  8.5 31.2 %collective-permute-start = (bf16[1,1,64,128]{3,2,1,0:T(8,128)(2,1)S(1)}, bf16[1,1,64,128]{3,2,1,0:T(8,128)(2,1)S(1)}, u32[]{:S(2)}, u32[]{:S(2)}) collective-permute-start(bf16[1,1,64,128]{3,2,1,0:T(8,128)(2,1)S(1)} %get-tuple-element.82), channel_id=1, source_target_pairs={{0,1},{1,2},{2,3},{3,4},{4,5},{5,6},{6,7},{7,0},{8,9},{9,10},{10,1... | collective-permute-start | bytes 49160 | tf_op jit(solution)/shard_map/ppermute | solution.py:16
  8.6 31.2 %collective-permute-start.1 = (bf16[1,1,64,128]{3,2,1,0:T(8,128)(2,1)S(1)}, bf16[1,1,64,128]{3,2,1,0:T(8,128)(2,1)S(1)}, u32[]{:S(2)}, u32[]{:S(2)}) collective-permute-start(bf16[1,1,64,128]{3,2,1,0:T(8,128)(2,1)S(1)} %get-tuple-element.83), channel_id=1, source_target_pairs={{1,0},{2,1},{3,2},{4,3},{5,4},{6,5},{7,6},{0,7},{9,8},{10,9},{11,1... | collective-permute-start | bytes 49160 | tf_op jit(solution)/shard_map/ppermute | solution.py:19
  78.3 8.8 %collective-permute-start.4 = (bf16[16,2,64,128]{3,0,2,1:T(8,128)(2,1)}, bf16[16,2,64,128]{3,0,2,1:T(8,128)(2,1)S(1)}, u32[]{:S(2)}, u32[]{:S(2)}) collective-permute-start(bf16[16,2,64,128]{3,0,2,1:T(8,128)(2,1)} %fusion.55), channel_id=1, source_target_pairs={{0,8},{8,16},{16,24},{24,0},{1,9},{9,17},{17,25},{25,1},{2,10},{10... | collective-permute-start | bytes 1572872 | tf_op jit(solution)/shard_map/ppermute | solution.py:27
  78.3 105.3 %copy-start.21 = (f32[16]{0:T(128)}, f32[16]{0:T(128)S(1)}, u32[]{:S(2)}) copy-start(f32[16]{0:T(128)S(1)} %get-tuple-element.92) | copy-start | bytes 196
  87.5 10.9 %collective-permute-start.5 = (bf16[16,1,64,128]{3,0,2,1:T(8,128)(2,1)S(1)}, bf16[16,1,64,128]{3,0,2,1:T(8,128)(2,1)S(1)}, u32[]{:S(2)}, u32[]{:S(2)}) collective-permute-start(bf16[16,1,64,128]{3,0,2,1:T(8,128)(2,1)S(1)} %get-tuple-element.46), channel_id=1, source_target_pairs={{0,1},{1,2},{2,3},{3,4},{4,5},{5,6},{6,7},{7,0},{8,9},{9,10},{10,1... | collective-permute-start | bytes 786440 | tf_op jit(solution)/shard_map/ppermute | solution.py:16
  87.5 13.3 %collective-permute-start.6 = (bf16[16,1,64,128]{3,0,2,1:T(8,128)(2,1)S(1)}, bf16[16,1,64,128]{3,0,2,1:T(8,128)(2,1)S(1)}, u32[]{:S(2)}, u32[]{:S(2)}) collective-permute-start(bf16[16,1,64,128]{3,0,2,1:T(8,128)(2,1)S(1)} %get-tuple-element.47), channel_id=1, source_target_pairs={{1,0},{2,1},{3,2},{4,3},{5,4},{6,5},{7,6},{0,7},{9,8},{10,9},{11,1... | collective-permute-start | bytes 786440 | tf_op jit(solution)/shard_map/ppermute | solution.py:19
  93.3 50.9 %copy-start.23 = (f32[2]{0:T(128)}, f32[2]{0:T(128)S(1)}, u32[]{:S(2)}) copy-start(f32[2]{0:T(128)S(1)} %get-tuple-element.89) | copy-start | bytes 28
  145.6 10.1 %collective-permute-start.7 = (bf16[1,1,64,128]{3,2,1,0:T(8,128)(2,1)S(1)}, bf16[1,1,64,128]{3,2,1,0:T(8,128)(2,1)S(1)}, u32[]{:S(2)}, u32[]{:S(2)}) collective-permute-start(bf16[1,1,64,128]{3,2,1,0:T(8,128)(2,1)S(1)} %get-tuple-element.80), channel_id=1, source_target_pairs={{0,1},{1,2},{2,3},{3,4},{4,5},{5,6},{6,7},{7,0},{8,9},{9,10},{10,1... | collective-permute-start | bytes 49160 | tf_op jit(solution)/shard_map/ppermute | solution.py:16
  145.6 10.1 %collective-permute-start.8 = (bf16[1,1,64,128]{3,2,1,0:T(8,128)(2,1)S(1)}, bf16[1,1,64,128]{3,2,1,0:T(8,128)(2,1)S(1)}, u32[]{:S(2)}, u32[]{:S(2)}) collective-permute-start(bf16[1,1,64,128]{3,2,1,0:T(8,128)(2,1)S(1)} %get-tuple-element.81), channel_id=1, source_target_pairs={{1,0},{2,1},{3,2},{4,3},{5,4},{6,5},{7,6},{0,7},{9,8},{10,9},{11,1... | collective-permute-start | bytes 49160 | tf_op jit(solution)/shard_map/ppermute | solution.py:19
  151.0 37.0 %collective-permute-start.11 = (bf16[1,1,64,128]{3,2,1,0:T(8,128)(2,1)}, bf16[1,1,64,128]{3,2,1,0:T(8,128)(2,1)S(1)}, u32[]{:S(2)}, u32[]{:S(2)}) collective-permute-start(bf16[1,1,64,128]{3,2,1,0:T(8,128)(2,1)} %get-tuple-element.76), channel_id=1, source_target_pairs={{0,1},{1,2},{2,3},{3,4},{4,5},{5,6},{6,7},{7,0},{8,9},{9,10},{10,1... | collective-permute-start | bytes 49160 | tf_op jit(solution)/shard_map/ppermute | solution.py:16
  151.0 37.0 %collective-permute-start.12 = (bf16[1,1,64,128]{3,2,1,0:T(8,128)(2,1)}, bf16[1,1,64,128]{3,2,1,0:T(8,128)(2,1)}, u32[]{:S(2)}, u32[]{:S(2)}) collective-permute-start(bf16[1,1,64,128]{3,2,1,0:T(8,128)(2,1)} %get-tuple-element.77), channel_id=1, source_target_pairs={{1,0},{2,1},{3,2},{4,3},{5,4},{6,5},{7,6},{0,7},{9,8},{10,9},{11,1... | collective-permute-start | bytes 49160 | tf_op jit(solution)/shard_map/ppermute | solution.py:19
  185.8 34.5 %collective-permute-start.10 = (bf16[16,1,64,128]{3,0,2,1:T(8,128)(2,1)}, bf16[16,1,64,128]{3,0,2,1:T(8,128)(2,1)S(1)}, u32[]{:S(2)}, u32[]{:S(2)}) collective-permute-start(bf16[16,1,64,128]{3,0,2,1:T(8,128)(2,1)} %get-tuple-element.45), channel_id=1, source_target_pairs={{1,0},{2,1},{3,2},{4,3},{5,4},{6,5},{7,6},{0,7},{9,8},{10,9},{11,1... | collective-permute-start | bytes 786440 | tf_op jit(solution)/shard_map/ppermute | solution.py:19
  187.1 33.2 %collective-permute-start.9 = (bf16[16,1,64,128]{3,0,2,1:T(8,128)(2,1)}, bf16[16,1,64,128]{3,0,2,1:T(8,128)(2,1)}, u32[]{:S(2)}, u32[]{:S(2)}) collective-permute-start(bf16[16,1,64,128]{3,0,2,1:T(8,128)(2,1)} %get-tuple-element.44), channel_id=1, source_target_pairs={{0,1},{1,2},{2,3},{3,4},{4,5},{5,6},{6,7},{7,0},{8,9},{9,10},{10,1... | collective-permute-start | bytes 786440 | tf_op jit(solution)/shard_map/ppermute | solution.py:16
  276.3 6.4 %collective-permute-start.13 = (bf16[1,1,64,128]{3,2,1,0:T(8,128)(2,1)S(1)}, bf16[1,1,64,128]{3,2,1,0:T(8,128)(2,1)S(1)}, u32[]{:S(2)}, u32[]{:S(2)}) collective-permute-start(bf16[1,1,64,128]{3,2,1,0:T(8,128)(2,1)S(1)} %get-tuple-element.78), channel_id=1, source_target_pairs={{0,1},{1,2},{2,3},{3,4},{4,5},{5,6},{6,7},{7,0},{8,9},{9,10},{10,1... | collective-permute-start | bytes 49160 | tf_op jit(solution)/shard_map/ppermute | solution.py:16
  276.3 6.4 %collective-permute-start.14 = (bf16[1,1,64,128]{3,2,1,0:T(8,128)(2,1)S(1)}, bf16[1,1,64,128]{3,2,1,0:T(8,128)(2,1)S(1)}, u32[]{:S(2)}, u32[]{:S(2)}) collective-permute-start(bf16[1,1,64,128]{3,2,1,0:T(8,128)(2,1)S(1)} %get-tuple-element.79), channel_id=1, source_target_pairs={{1,0},{2,1},{3,2},{4,3},{5,4},{6,5},{7,6},{0,7},{9,8},{10,9},{11,1... | collective-permute-start | bytes 49160 | tf_op jit(solution)/shard_map/ppermute | solution.py:19
  315.0 8.8 %collective-permute-start.15 = (bf16[16,2,64,128]{3,0,2,1:T(8,128)(2,1)}, bf16[16,2,64,128]{3,0,2,1:T(8,128)(2,1)S(1)}, u32[]{:S(2)}, u32[]{:S(2)}) collective-permute-start(bf16[16,2,64,128]{3,0,2,1:T(8,128)(2,1)} %fusion.53), channel_id=1, source_target_pairs={{0,8},{8,16},{16,24},{24,0},{1,9},{9,17},{17,25},{25,1},{2,10},{10... | collective-permute-start | bytes 1572872 | tf_op jit(solution)/shard_map/ppermute | solution.py:27
  324.2 9.5 %collective-permute-start.16 = (bf16[16,1,64,128]{3,0,2,1:T(8,128)(2,1)S(1)}, bf16[16,1,64,128]{3,0,2,1:T(8,128)(2,1)S(1)}, u32[]{:S(2)}, u32[]{:S(2)}) collective-permute-start(bf16[16,1,64,128]{3,0,2,1:T(8,128)(2,1)S(1)} %get-tuple-element.42), channel_id=1, source_target_pairs={{0,1},{1,2},{2,3},{3,4},{4,5},{5,6},{6,7},{7,0},{8,9},{9,10},{10,1... | collective-permute-start | bytes 786440 | tf_op jit(solution)/shard_map/ppermute | solution.py:16
  324.2 12.0 %collective-permute-start.17 = (bf16[16,1,64,128]{3,0,2,1:T(8,128)(2,1)S(1)}, bf16[16,1,64,128]{3,0,2,1:T(8,128)(2,1)S(1)}, u32[]{:S(2)}, u32[]{:S(2)}) collective-permute-start(bf16[16,1,64,128]{3,0,2,1:T(8,128)(2,1)S(1)} %get-tuple-element.43), channel_id=1, source_target_pairs={{1,0},{2,1},{3,2},{4,3},{5,4},{6,5},{7,6},{0,7},{9,8},{10,9},{11,1... | collective-permute-start | bytes 786440 | tf_op jit(solution)/shard_map/ppermute | solution.py:19
  380.2 6.4 %collective-permute-start.18 = (bf16[1,1,64,128]{3,2,1,0:T(8,128)(2,1)S(1)}, bf16[1,1,64,128]{3,2,1,0:T(8,128)(2,1)S(1)}, u32[]{:S(2)}, u32[]{:S(2)}) collective-permute-start(bf16[1,1,64,128]{3,2,1,0:T(8,128)(2,1)S(1)} %get-tuple-element.74), channel_id=1, source_target_pairs={{0,1},{1,2},{2,3},{3,4},{4,5},{5,6},{6,7},{7,0},{8,9},{9,10},{10,1... | collective-permute-start | bytes 49160 | tf_op jit(solution)/shard_map/ppermute | solution.py:16
  380.2 6.4 %collective-permute-start.19 = (bf16[1,1,64,128]{3,2,1,0:T(8,128)(2,1)S(1)}, bf16[1,1,64,128]{3,2,1,0:T(8,128)(2,1)S(1)}, u32[]{:S(2)}, u32[]{:S(2)}) collective-permute-start(bf16[1,1,64,128]{3,2,1,0:T(8,128)(2,1)S(1)} %get-tuple-element.75), channel_id=1, source_target_pairs={{1,0},{2,1},{3,2},{4,3},{5,4},{6,5},{7,6},{0,7},{9,8},{10,9},{11,1... | collective-permute-start | bytes 49160 | tf_op jit(solution)/shard_map/ppermute | solution.py:19
  416.0 9.2 %collective-permute-start.20 = (bf16[16,1,64,128]{3,0,2,1:T(8,128)(2,1)S(1)}, bf16[16,1,64,128]{3,0,2,1:T(8,128)(2,1)S(1)}, u32[]{:S(2)}, u32[]{:S(2)}) collective-permute-start(bf16[16,1,64,128]{3,0,2,1:T(8,128)(2,1)S(1)} %get-tuple-element.40), channel_id=1, source_target_pairs={{0,1},{1,2},{2,3},{3,4},{4,5},{5,6},{6,7},{7,0},{8,9},{9,10},{10,1... | collective-permute-start | bytes 786440 | tf_op jit(solution)/shard_map/ppermute | solution.py:16
  416.1 10.0 %collective-permute-start.21 = (bf16[16,1,64,128]{3,0,2,1:T(8,128)(2,1)S(1)}, bf16[16,1,64,128]{3,0,2,1:T(8,128)(2,1)S(1)}, u32[]{:S(2)}, u32[]{:S(2)}) collective-permute-start(bf16[16,1,64,128]{3,0,2,1:T(8,128)(2,1)S(1)} %get-tuple-element.41), channel_id=1, source_target_pairs={{1,0},{2,1},{3,2},{4,3},{5,4},{6,5},{7,6},{0,7},{9,8},{10,9},{11,1... | collective-permute-start | bytes 786440 | tf_op jit(solution)/shard_map/ppermute | solution.py:19
  (42 other events, 319.8 us)
where the time goes:
time: 506 us; the launch traced here: 497 us
  local copies, waits for them, and re-layouts  187 us (37%)
  matrix products  167 us (33%)
  starting transfers between devices  46.6 us (9%)
  other arithmetic  36.3 us (7%)
  waiting for transfers between devices  32.6 us (6%)
  blocking collectives  22 us (4%)
  between operations  6.19 us (1%)
    conv_general_dilated x10, matrix products, conv_slab(): lax.conv_general_dilated(widened[None], kernel, (1, 1, 1), 'VALID', dimen...  163 us
    conv_general_dilated x36, local copies, waits for them, and re-layouts, conv_slab(): lax.conv_general_dilated(widened[None], kernel, (1, 1, 1), 'VALID', dimen...  131 us
    ppermute x10, starting transfers between devices, with_halo(): lax.ppermute(lax.slice_in_dim(block, 0, width, axis=dim), axis, backward)  42.4 us
    unnamed x108, local copies, waits for them, and re-layouts  39 us
    psum x1, blocking collectives, shards(): whole = lax.psum(total, 'space')  22 us
    ppermute x10, waiting for transfers between devices, with_halo(): lax.ppermute(lax.slice_in_dim(block, block.shape[dim] - width, None, axis...  17.2 us
    broadcast_in_dim x5, other arithmetic, conv_slab(): widened[None]  12.1 us
  transfers between devices with their start and end apart: 22, of which 10 were waited for; matrix products, arithmetic and copies ran while one was open for 20% of the time, Pallas kernels for 0%

commit v1 on v0

v1 whole, which is shorter than its diff:
```python
import functools

import jax
import jax.numpy as jnp
from jax import lax
from jax.experimental import pallas as pl
from jax.experimental.pallas import tpu as pltpu
from jax.sharding import PartitionSpec as P

LAYERS = 2
TICKS = 2
CH = 16
BF = jnp.bfloat16
F32 = jnp.float32

PX = 2
HALO = 4
FX = PX + 2 * HALO
HX0 = FX - 2
GR = 32
BY = 4


def one_hot(shape, fn):
    row = lax.broadcasted_iota(jnp.int32, shape, 0)
    col = lax.broadcasted_iota(jnp.int32, shape, 1)
    return jnp.where(fn(row, col), 1.0, 0.0).astype(BF)


def exact_dot(a, b):
    return jnp.dot(a, b, preferred_element_type=F32)


def col_dot(a, b):
    return lax.dot_general(a, b, (((0,), (0,)), ((), ())), preferred_element_type=F32)


def split2(value):
    high = value.astype(BF)
    low = (value - high.astype(F32)).astype(BF)
    return jnp.concatenate([high, low], axis=0)


def prep_kernel(enc_ref, enc_b_ref, in_ref, hid_b_ref, ctx_ref, mid_ref, mid_b_ref, out_ref,
                wenc_ref, win0_ref, win1_ref, wctx_ref, wmid_ref, bmid_ref, wout_ref):
    lanes = 2 * 128

    def taps(load):
        return jnp.concatenate([load(k) for k in range(9)], axis=0)

    def banded(rows27, bias2, planes, shift0, dst):
        def place(row, col):
            dx, dy, dz = row // 9, (row // 3) % 3, row % 3
            return col == dy * GR + dz * FX + dx
        base = col_dot(rows27, one_hot((27, lanes), place))
        extra = col_dot(bias2, one_hot((2, lanes), lambda row, col: col == 3 * FX + row))
        for y in range(BY):
            for x in range(planes):
                shift = y * GR + x + shift0
                moved = base if shift == 0 else pltpu.roll(base, shift, 1)
                r = (y * planes + x) * CH
                dst[r:r + CH, :] = (moved + extra).astype(BF)

    banded(taps(lambda k: enc_ref[k].astype(F32)).astype(BF), split2(enc_b_ref[...]), HX0, 0, wenc_ref)
    for layer, (dst, planes, shift0) in enumerate(((win0_ref, HX0, 0), (win1_ref, HX0 - 4, 2))):
        rows = taps(lambda k: in_ref[k, :, layer, :].astype(F32)).astype(BF)
        banded(rows, split2(hid_b_ref[layer:layer + 1, :]), planes, shift0, dst)

    spread = one_hot((CH, 256), lambda row, col: col % CH == row)
    row = lax.broadcasted_iota(jnp.int32, (256, 256), 0)
    col = lax.broadcasted_iota(jnp.int32, (256, 256), 1)
    for layer in range(LAYERS):
        wide = exact_dot(ctx_ref[layer], spread)
        tall = jnp.concatenate([wide] * 16, axis=0)
        wctx_ref[layer] = jnp.where(row // CH == col // CH, tall, 0.0).astype(BF)
        narrow = exact_dot(out_ref[layer], spread)
        for o in range(2):
            line = jnp.broadcast_to(narrow[o:o + 1, :], (16, 256))
            r = row[:16] % 8 * 2 + row[:16] // 8
            wout_ref[layer, o * 16:o * 16 + 16, :] = jnp.where(col[:16] // CH == r, line, 0.0).astype(BF)
        bias2 = split2(mid_b_ref[layer:layer + 1, :])
        bmid_ref[layer] = col_dot(bias2, jnp.ones((2, 128), BF))
        zero = jnp.zeros((CH, CH), F32)
        for dz in range(3):
            pieces = []
            for dy in range(3):
                for dx in range(3):
                    pieces.append(mid_ref[layer, (dx * 3 + dy) * 3 + dz].astype(F32))
                pieces.append(zero)
            base = jnp.concatenate(pieces + [zero] * 12, axis=1)
            for y in range(BY):
                for x in range(2):
                    shift = (y * 4 + x) * CH
                    moved = base if shift == 0 else pltpu.roll(base, shift, 1)
                    r = (y * 2 + x) * CH
                    wmid_ref[layer, r:r + CH, dz * 384:dz * 384 + 384] = moved.astype(BF)


def tick_kernel(tick, lines, prev_refs, base_refs, mask_ref, wenc_ref, win0_ref, win1_ref, wctx_ref,
                wmid_ref, bmid_ref, wout_ref, out_b_ref, phi_ref, send_ref, sum_ref, g_ref, gb_ref, c_ref,
                h_ref, keep_ref):
    steps = lines // (2 * BY)
    nz = 128

    def gather_plane(p, first, value):
        rows = value.shape[0]
        for dz in range(3):
            moved = value if dz == 1 else pltpu.roll(value, 1 if dz == 0 else nz - 1, 1)
            g_ref[pl.ds(first * GR + dz * FX + p, rows, stride=GR), :] = moved

    def gather_done():
        for line in range(lines):
            gb_ref[(line + 1) * GR:(line + 2) * GR, :] = g_ref[line * GR:(line + 1) * GR, :].astype(BF)
        gb_ref[0:GR, :] = gb_ref[lines * GR:(lines + 1) * GR, :]
        gb_ref[(lines + 1) * GR:(lines + 2) * GR, :] = gb_ref[GR:2 * GR, :]

    def window(y0):
        left = gb_ref[y0 * GR:(y0 + BY + 2) * GR, :]
        right = gb_ref[(y0 + BY) * GR:(y0 + 2 * BY + 2) * GR, :]
        return jnp.concatenate([left, right], axis=1)

    def store_hidden(y, value, size):
        count = value.shape[0] // size
        for dz in range(3):
            moved = value if dz == 1 else pltpu.roll(value, 1 if dz == 0 else nz - 1, 1)
            h_ref[dz, y + 1:y + 1 + count, 0:size, :] = moved.astype(BF).reshape(count, size, nz)

    def wrap_hidden(size):
        for dz in range(3):
            h_ref[dz, 0, 0:size, :] = h_ref[dz, lines, 0:size, :]
            h_ref[dz, lines + 1, 0:size, :] = h_ref[dz, 1, 0:size, :]

    kin = (BY + 2) * GR

    ones = jnp.ones((lines, nz), F32)
    for k in range(2):
        g_ref[pl.ds(3 * FX + k, lines, stride=GR), :] = ones

    for k, ref in enumerate(prev_refs):
        for j in range(PX):
            gather_plane(k * PX + j, 0, ref[j].astype(F32))
    gather_done()
    size = HX0 * CH
    for i in range(steps):
        y0 = i * 2 * BY
        rhs = window(y0)
        for part in range(2):
            w = wenc_ref[part * 256:part * 256 + 256, 0:kin]
            value = jnp.tanh(exact_dot(w, rhs)).astype(BF)
            for half in range(2):
                y = y0 + half * BY + part * 2
                c_ref[y:y + 2] = value[:, half * nz:half * nz + nz].reshape(2, size, nz)

    def start_plane(p, layer):
        k, j = divmod(p, PX)
        ref = base_refs[k]
        return ref[tick, j].astype(F32)

    for p in range(FX):
        gather_plane(p, 0, mask_ref[0, p % PX].astype(F32) * start_plane(p, 0))
    gather_done()
    for i in range(steps):
        y0 = i * 2 * BY
        rhs = window(y0)
        for part in range(2):
            y = y0 + part * 2
            ctx = jnp.concatenate(
                [c_ref[y:y + 2].reshape(256, nz), c_ref[y + BY:y + BY + 2].reshape(256, nz)], axis=1
            )
            first = exact_dot(win0_ref[part * 256:part * 256 + 256, 0:kin], rhs) + exact_dot(wctx_ref[0], ctx)
            value = jnp.tanh(first)
            for half in range(2):
                store_hidden(y + half * BY, value[:, half * nz:half * nz + nz], size)
    wrap_hidden(size)

    def middle(layer, y0, x0):
        parts = []
        for dz in range(3):
            side = []
            for half in range(2):
                y = y0 + half * BY
                block = h_ref[dz, y:y + BY + 2, x0 * CH:(x0 + 4) * CH, :]
                side.append(block.reshape((BY + 2) * 4 * CH, nz))
            parts.append(jnp.concatenate(side, axis=1))
        second = exact_dot(wmid_ref[layer], jnp.concatenate(parts, axis=0))
        bias = jnp.concatenate([bmid_ref[layer]] * 8, axis=0)
        second = second + jnp.concatenate([bias, bias], axis=1)
        deeper = jnp.tanh(second).astype(BF)
        return jnp.concatenate([deeper[:, :nz], deeper[:, nz:]], axis=0)

    def couple(layer, keep, phi, o0, o1):
        scale = jnp.tanh(o0 + out_b_ref[layer, 0])
        drop = 1.0 - keep
        moved = keep * phi + drop * (phi * jnp.exp(scale) + (o1 + out_b_ref[layer, 1]))
        return moved, drop * scale

    total = jnp.zeros((8, nz), F32)
    for i in range(steps):
        y0 = i * 2 * BY
        rows = slice(y0, y0 + 2 * BY)
        deep = jnp.concatenate([middle(0, y0, x0) for x0 in (0, 2, 4)], axis=1)
        o = exact_dot(wout_ref[0], deep)
        for j in range(6):
            p = j + 2
            k, jj = divmod(p, PX)
            lane = slice((j // 2) * nz, (j // 2) * nz + nz)
            r = (j % 2) * 8
            keep = mask_ref[0, p % PX, rows, :].astype(F32)
            phi = base_refs[k][tick, jj, rows, :].astype(F32)
            phi, part = couple(0, keep, phi, o[r:r + 8, lane], o[16 + r:24 + r, lane])
            if k == 2:
                keep_ref[jj, rows, :] = phi
                total = total + part
            gather_plane(p, y0, mask_ref[1, p % PX, rows, :].astype(F32) * phi)

    gather_done()
    size1 = (HX0 - 4) * CH
    for i in range(steps):
        y0 = i * 2 * BY
        ctx = jnp.concatenate(
            [c_ref[y:y + BY, 2 * CH:6 * CH, :].reshape(256, nz) for y in (y0, y0 + BY)], axis=1
        )
        first = exact_dot(win1_ref[:, 0:kin], window(y0)) + exact_dot(wctx_ref[1], ctx)
        value = jnp.tanh(first)
        for half in range(2):
            store_hidden(y0 + half * BY, value[:, half * nz:half * nz + nz], size1)
    wrap_hidden(size1)
    for i in range(steps):
        y0 = i * 2 * BY
        rows = slice(y0, y0 + 2 * BY)
        o = exact_dot(wout_ref[1], middle(1, y0, 0))
        for j in range(PX):
            keep = mask_ref[1, j, rows, :].astype(F32)
            r = j * 8
            phi, part = couple(1, keep, keep_ref[j, rows, :], o[r:r + 8], o[16 + r:24 + r])
            phi_ref[j, rows, :] = phi
            if send_ref is not None:
                send_ref[j, rows, :] = phi.astype(BF)
            total = total + part
    sum_ref[...] = jnp.broadcast_to(jnp.sum(total, axis=0, keepdims=True), (8, nz))


VMEM = pl.BlockSpec(memory_space=pltpu.VMEM)
SMEM = pl.BlockSpec(memory_space=pltpu.SMEM)


def prepare(enc_w, enc_b, in_w, hid_b, ctx_w, mid_w, mid_b, out_w):
    enc = jnp.transpose(enc_w, (1, 2, 3, 4, 0)).reshape(9, 3, CH)
    inw = jnp.transpose(in_w, (2, 3, 4, 5, 0, 1)).reshape(9, 3, LAYERS, CH)
    mid = jnp.transpose(mid_w, (0, 3, 4, 5, 1, 2)).reshape(LAYERS, 27, CH, CH)
    shapes = (
        (BY * HX0 * CH, 256), (BY * HX0 * CH, 256), (BY * (HX0 - 4) * CH, 256),
        (LAYERS, 256, 256), (LAYERS, BY * 2 * CH, 3 * 384), None, (LAYERS, 32, 256),
    )
    out_shape = [
        jax.ShapeDtypeStruct((LAYERS, CH, 128), F32) if s is None else jax.ShapeDtypeStruct(s, BF)
        for s in shapes
    ]
    return pl.pallas_call(
        prep_kernel,
        out_shape=out_shape,
        in_specs=[VMEM] * 8,
        out_specs=[VMEM] * 7,
        name="prep",
    )(enc, enc_b.reshape(1, CH), inw, hid_b, ctx_w, mid, mid_b, out_w)


def run_tick(tick, prevs, bases, masks, weights, out_b):
    lines, nz = masks.shape[2], masks.shape[3]
    last = tick == TICKS - 1

    def body(*refs):
        prev, rest = refs[:5], refs[5:]
        base, rest = rest[:5], rest[5:]
        mask, rest = rest[0], rest[1:]
        w, rest = rest[:7], rest[7:]
        out_b_ref, rest = rest[0], rest[1:]
        if last:
            phi, total = rest[:2]
            send, scratch = None, rest[2:]
        else:
            phi, send, total = rest[:3]
            scratch = rest[3:]
        tick_kernel(tick, lines, prev, base, mask, *w, out_b_ref, phi, send, total, *scratch)

    out_shape = [jax.ShapeDtypeStruct((PX, lines, nz), F32)]
    if not last:
        out_shape.append(jax.ShapeDtypeStruct((PX, lines, nz), BF))
    out_shape.append(jax.ShapeDtypeStruct((8, nz), F32))
    return pl.pallas_call(
        body,
        out_shape=out_shape,
        in_specs=[VMEM] * (5 + 5 + 1 + 7) + [SMEM],
        out_specs=[VMEM] * len(out_shape),
        scratch_shapes=[
            pltpu.VMEM((lines * GR, nz), F32),
            pltpu.VMEM(((lines + 2) * GR, nz), BF),
            pltpu.VMEM((lines, HX0 * CH, nz), BF),
            pltpu.VMEM((3, lines + 2, HX0 * CH, nz), BF),
            pltpu.VMEM((PX, lines, nz), F32),
        ],
        name=f"tick{tick}",
    )(*prevs, *bases, masks, *weights, out_b)


def shards(base, phi_prev, masks, enc_w, enc_b, in_w, ctx_w, hid_b, mid_w, mid_b, out_w, out_b):
    nt, ns = lax.axis_size("tm"), lax.axis_size("space")
    sites_total = masks.shape[1] * masks.shape[2] * masks.shape[3] * ns

    def moved(value, dt, ds):
        pairs = [
            (t * ns + s, (t + dt) % nt * ns + (s + ds) % ns) for t in range(nt) for s in range(ns)
        ]
        return lax.ppermute(value, ("tm", "space"), pairs)

    def around(value, dt):
        return [moved(value, dt, ds) if dt or ds else value for ds in (2, 1, 0, -1, -2)]

    start = base[:, 0]
    starts = around(start.astype(BF), 0)
    starts[2] = start
    prevs = around(phi_prev[0].astype(BF), 1)
    weights = prepare(enc_w, enc_b, in_w, hid_b, ctx_w, mid_w, mid_b, out_w)
    phi0, send, sum0 = run_tick(0, prevs, starts, masks, weights, out_b)
    phi1, sum1 = run_tick(1, around(send, 1), starts, masks, weights, out_b)
    total = jnp.stack([jnp.sum(sum0[0]), jnp.sum(sum1[0])])
    total = jnp.broadcast_to(total[:, None], (2, 128))
    step = 1
    while step < ns:
        pairs = [(s, s ^ step) for s in range(ns)]
        total = total + lax.ppermute(total, "space", pairs)
        step *= 2
    return (jnp.stack([phi0, phi1])[:, None], total[:, :1] / sites_total)


def solution(mesh):
    in_specs = (
        P(None, "tm", "space", None, None),
        P("tm", "space", None, None),
        P(None, "space", None, None),
        P(), P(), P(), P(), P(), P(), P(), P(), P(),
    )
    out_specs = (P(None, "tm", "space", None, None), P(None, "tm"))
    return jax.shard_map(shards, mesh=mesh, in_specs=in_specs, out_specs=out_specs, check_vma=False)
```

time: 506 us -> 79.2 us (0.16); the launches traced: 497 us -> 78.8 us
  local copies, waits for them, and re-layouts: 187 us -> 1.91 us
  matrix products: 167 us -> 0 us
  other arithmetic: 36.3 us -> 7 us
  Pallas kernels: 0 us -> 28.3 us
  starting transfers between devices: 46.6 us -> 21.6 us
  blocking collectives: 22 us -> 0 us
  waiting for transfers between devices: 32.6 us -> 19.3 us
  between operations: 6.19 us -> 0.8 us
    conv_general_dilated x10 -> x0, matrix products: 163 us -> none  [conv_slab(): lax.conv_general_dilated(widened[None], kernel, (1, 1, 1), 'VALID', dimen...]
    conv_general_dilated x36 -> x0, local copies, waits for them, and re-layouts: 131 us -> none  [conv_slab(): lax.conv_general_dilated(widened[None], kernel, (1, 1, 1), 'VALID', dimen...]
    unnamed x108 -> x32, local copies, waits for them, and re-layouts: 39 us -> 1.9 us
    pallas_call x0 -> x3, Pallas kernels: none -> 28.3 us  [the longest x2 25.4 us: run_tick(): pl.pallas_call(body, out_shape=out_shape, in_specs=[VMEM] * (5 + 5 + 1 +...]
    ppermute x22 -> x17, starting transfers between devices: 46.6 us -> 21.6 us  [the longest x14 19.8 us: moved(): return lax.ppermute(value, ('tm', 'space'), pairs)]
    psum x1 -> x0, blocking collectives: 22 us -> none  [shards(): whole = lax.psum(total, 'space')]
    ppermute x22 -> x17, waiting for transfers between devices: 32.6 us -> 19.3 us  [the longest x3 11.5 us: shards(): total = total + lax.ppermute(total, 'space', pairs)]
    broadcast_in_dim x6 -> x0, other arithmetic: 12.7 us -> none  [the longest x5 12.1 us: conv_slab(): widened[None]]
  transfers between devices with their start and end apart: 22 -> 17, of which waited for: 10 -> 6; matrix products, arithmetic and copies ran while one was open for 20% -> 4% of each run, Pallas kernels for 0% -> 4%
where the time goes in v1:
time: 79.2 us; the launch traced here: 78.8 us
  Pallas kernels  28.3 us (36%)
  starting transfers between devices  21.6 us (27%)
  waiting for transfers between devices  19.3 us (24%)
  other arithmetic  7 us (9%)
  local copies, waits for them, and re-layouts  1.91 us (2%)
  between operations  0.8 us (1%)
    pallas_call x2, Pallas kernels, run_tick(): pl.pallas_call(body, out_shape=out_shape, in_specs=[VMEM] * (5 + 5 + 1 +...  25.4 us
    ppermute x14, starting transfers between devices, moved(): return lax.ppermute(value, ('tm', 'space'), pairs)  19.8 us
    ppermute x3, waiting for transfers between devices, shards(): total = total + lax.ppermute(total, 'space', pairs)  11.5 us
    ppermute x14, waiting for transfers between devices, moved(): return lax.ppermute(value, ('tm', 'space'), pairs)  7.76 us
    pallas_call x1, Pallas kernels, prepare(): pl.pallas_call(prep_kernel, out_shape=out_shape, in_specs=[VMEM] * 8, out...  2.92 us
    reduce_sum x2, other arithmetic, shards(): total = jnp.stack([jnp.sum(sum0[0]), jnp.sum(sum1[0])])  2.63 us
    unnamed x32, local copies, waits for them, and re-layouts  1.9 us
    ppermute x3, starting transfers between devices, shards(): total = total + lax.ppermute(total, 'space', pairs)  1.77 us
  transfers between devices with their start and end apart: 17, of which 6 were waited for; matrix products, arithmetic and copies ran while one was open for 4% of the time, Pallas kernels for 4%

profile of v1, /device:TPU:0, one launch (start us, length us, event | category | flops | bytes accessed | tf_op | source)
XLA Modules:
  0.0 78.8 jit_solution(4358950798466286009)
XLA Ops:
  0.6 0.8 %convert_bitcast_fusion = bf16[2,64,128]{2,1,0:T(8,128)(2,1)S(1)} fusion(f32[1,2,64,128]{3,2,1,0:T(8,128)} %param.13), kind=kLoop, calls=%fused_computation.2 | loop fusion | flops 16384 | bytes 98304 | tf_op jit(solution)/shard_map/convert_element_type | solution.py:322
  1.5 4.5 %collective-permute-start.4 = (bf16[2,64,128]{2,1,0:T(8,128)(2,1)S(1)}, bf16[2,64,128]{2,1,0:T(8,128)(2,1)S(1)}, u32[]{:S(2)}, u32[]{:S(2)}) collective-permute-start(bf16[2,64,128]{2,1,0:T(8,128)(2,1)S(1)} %convert_bitcast_fusion), channel_id=1, source_target_pairs={{0,14},{1,15},{2,8},{3,9},{4,10},{5,11},{6,12},{7,13},{8,22},{9,23... | collective-permute-start | bytes 98312 | tf_op jit(solution)/shard_map/ppermute | solution.py:314
  6.0 2.6 %collective-permute-start.3 = (bf16[2,64,128]{2,1,0:T(8,128)(2,1)S(1)}, bf16[2,64,128]{2,1,0:T(8,128)(2,1)S(1)}, u32[]{:S(2)}, u32[]{:S(2)}) collective-permute-start(bf16[2,64,128]{2,1,0:T(8,128)(2,1)S(1)} %convert_bitcast_fusion), channel_id=1, source_target_pairs={{0,15},{1,8},{2,9},{3,10},{4,11},{5,12},{6,13},{7,14},{8,23},{9,16... | collective-permute-start | bytes 98312 | tf_op jit(solution)/shard_map/ppermute | solution.py:314
  8.6 0.9 %collective-permute-start.1 = (bf16[2,64,128]{2,1,0:T(8,128)(2,1)S(1)}, bf16[2,64,128]{2,1,0:T(8,128)(2,1)S(1)}, u32[]{:S(2)}, u32[]{:S(2)}) collective-permute-start(bf16[2,64,128]{2,1,0:T(8,128)(2,1)S(1)} %convert_bitcast_fusion), channel_id=1, source_target_pairs={{0,9},{1,10},{2,11},{3,12},{4,13},{5,14},{6,15},{7,8},{8,17},{9,18... | collective-permute-start | bytes 98312 | tf_op jit(solution)/shard_map/ppermute | solution.py:314
  9.5 0.9 %bitcast_convert_fusion = bf16[2,2,64,128]{3,2,1,0:T(8,128)(2,1)S(1)} fusion(f32[2,1,2,64,128]{4,3,2,1,0:T(8,128)} %param.12), kind=kLoop, calls=%fused_computation.8 | loop fusion | flops 32768 | bytes 196608 | tf_op jit(solution)/shard_map/convert_element_type | solution.py:320
  10.9 3.7 %collective-permute-start.7 = (bf16[2,2,64,128]{3,2,1,0:T(8,128)(2,1)S(1)}, bf16[2,2,64,128]{3,2,1,0:T(8,128)(2,1)S(1)}, u32[]{:S(2)}, u32[]{:S(2)}) collective-permute-start(bf16[2,2,64,128]{3,2,1,0:T(8,128)(2,1)S(1)} %bitcast_convert_fusion), channel_id=1, source_target_pairs={{0,7},{1,0},{2,1},{3,2},{4,3},{5,4},{6,5},{7,6},{8,15},{9,8},{10,9... | collective-permute-start | bytes 196616 | tf_op jit(solution)/shard_map/ppermute | solution.py:314
  15.2 1.5 %collective-permute-start.5 = (bf16[2,2,64,128]{3,2,1,0:T(8,128)(2,1)S(1)}, bf16[2,2,64,128]{3,2,1,0:T(8,128)(2,1)S(1)}, u32[]{:S(2)}, u32[]{:S(2)}) collective-permute-start(bf16[2,2,64,128]{3,2,1,0:T(8,128)(2,1)S(1)} %bitcast_convert_fusion), channel_id=1, source_target_pairs={{0,2},{1,3},{2,4},{3,5},{4,6},{5,7},{6,0},{7,1},{8,10},{9,11},{10,... | collective-permute-start | bytes 196616 | tf_op jit(solution)/shard_map/ppermute | solution.py:314
  16.7 2.9 %prep.1 = (bf16[512,256]{1,0:T(8,128)(2,1)}, bf16[512,256]{1,0:T(8,128)(2,1)}, bf16[256,256]{1,0:T(8,128)(2,1)}, bf16[2,256,256]{2,1,0:T(8,128)(2,1)}, bf16[2,12...) custom-call(bf16[9,3,16]{2,1,0:T(4,128)(2,1)} %bitcast.28, f32[1,16]{1,0:T(1,128)} %bitcast.29, ...), custom_call_target="tpu_custom_call" | custom-call | tf_op jit(solution)/shard_map/prep/pallas_call | solution.py:259
  19.6 3.3 %collective-permute-done.refs_0_ = bf16[2,64,128]{2,1,0:T(8,128)(2,1)S(1)} collective-permute-done((bf16[2,64,128]{2,1,0:T(8,128)(2,1)S(1)}, bf16[2,64,128]{2,1,0:T(8,128)(2,1)S(1)}, u32[]{:S(2)}, u32[]{:S(2)}) %collective-permute-start) | collective-permute-done | bytes 32800 | tf_op jit(solution)/shard_map/ppermute | solution.py:314
  23.6 12.7 %tick0.1 = (f32[2,64,128]{2,1,0:T(8,128)}, bf16[2,64,128]{2,1,0:T(8,128)(2,1)}, f32[8,128]{1,0:T(8,128)}) custom-call(bf16[2,64,128]{2,1,0:T(8,128)(2,1)} %copy-done.15, bf16[2,64,128]{2,1,0:T(8,128)(2,1)} %copy-done.9, bf16[2,64,128]{2,1,0:T(8,128)(2,1)} %copy-done.8, bf16[2,64,128]{2,1,0:T(8,128)(2,1)} %copy-done.7, bf16[2,64,128]{2,1,0:T(8,128)(2,1)} %copy-done.6, ...), custom_call_target="tpu_custom_call" | custom-call | tf_op jit(solution)/shard_map/tick0/pallas_call | solution.py:290
  36.3 1.2 %collective-permute-start.13 = (bf16[2,64,128]{2,1,0:T(8,128)(2,1)}, bf16[2,64,128]{2,1,0:T(8,128)(2,1)S(1)}, u32[]{:S(2)}, u32[]{:S(2)}) collective-permute-start(bf16[2,64,128]{2,1,0:T(8,128)(2,1)} %get-tuple-element.22), channel_id=1, source_target_pairs={{0,14},{1,15},{2,8},{3,9},{4,10},{5,11},{6,12},{7,13},{8,22},{9,23... | collective-permute-start | bytes 98312 | tf_op jit(solution)/shard_map/ppermute | solution.py:314
  37.5 2.2 %collective-permute-start.12 = (bf16[2,64,128]{2,1,0:T(8,128)(2,1)}, bf16[2,64,128]{2,1,0:T(8,128)(2,1)S(1)}, u32[]{:S(2)}, u32[]{:S(2)}) collective-permute-start(bf16[2,64,128]{2,1,0:T(8,128)(2,1)} %get-tuple-element.22), channel_id=1, source_target_pairs={{0,15},{1,8},{2,9},{3,10},{4,11},{5,12},{6,13},{7,14},{8,23},{9,16... | collective-permute-start | bytes 98312 | tf_op jit(solution)/shard_map/ppermute | solution.py:314
  39.7 0.7 collective-permute-start.11
  40.5 1.5 %collective-permute-start.9 = (bf16[2,64,128]{2,1,0:T(8,128)(2,1)}, bf16[2,64,128]{2,1,0:T(8,128)(2,1)S(1)}, u32[]{:S(2)}, u32[]{:S(2)}) collective-permute-start(bf16[2,64,128]{2,1,0:T(8,128)(2,1)} %get-tuple-element.22), channel_id=1, source_target_pairs={{0,10},{1,11},{2,12},{3,13},{4,14},{5,15},{6,8},{7,9},{8,18},{9,19... | collective-permute-start | bytes 98312 | tf_op jit(solution)/shard_map/ppermute | solution.py:314
  41.9 1.3 %slice_reduce_fusion.1 = f32[]{:T(128)} fusion(f32[8,128]{1,0:T(8,128)} %get-tuple-element.24), kind=kLoop, calls=%fused_computation.7 | loop fusion | flops 127 | bytes 516 | tf_op jit(solution)/shard_map/reduce_sum | solution.py:326
  43.4 4.3 %collective-permute-done.10.refs_1_ = bf16[2,64,128]{2,1,0:T(8,128)(2,1)S(1)} collective-permute-done((bf16[2,64,128]{2,1,0:T(8,128)(2,1)}, bf16[2,64,128]{2,1,0:T(8,128)(2,1)S(1)}, u32[]{:S(2)}, u32[]{:S(2)}) %collective-permute-start.10) | collective-permute-done | bytes 32800 | tf_op jit(solution)/shard_map/ppermute | solution.py:314
  48.9 12.7 %tick1.1 = (f32[2,64,128]{2,1,0:T(8,128)}, f32[8,128]{1,0:T(8,128)}) custom-call(bf16[2,64,128]{2,1,0:T(8,128)(2,1)} %copy-done.14, bf16[2,64,128]{2,1,0:T(8,128)(2,1)} %copy-done.13, bf16[2,64,128]{2,1,0:T(8,128)(2,1)} %copy-done.12, bf16[2,64,128]{2,1,0:T(8,128)(2,1)} %copy-done.11, bf16[2,64,128]{2,1,0:T(8,128)(2,1)} %copy-done.10, ...), custom_call_target="tpu_custom_call" | custom-call | tf_op jit(solution)/shard_map/tick1/pallas_call | solution.py:290
  61.6 1.3 %slice_reduce_fusion = f32[]{:T(128)} fusion(f32[8,128]{1,0:T(8,128)} %get-tuple-element.25), kind=kLoop, calls=%fused_computation.6 | loop fusion | flops 127 | bytes 516 | tf_op jit(solution)/shard_map/reduce_sum | solution.py:326
  62.9 1.4 %pad_maximum_fusion = f32[2]{0:T(128)S(1)} fusion(f32[1]{0:T(128)} %bitcast.14, f32[1]{0:T(128)} %bitcast.13), kind=kLoop, calls=%fused_computation.5 | loop fusion | flops 2 | bytes 16 | tf_op jit(solution)/shard_map/stack | solution.py:326
  64.3 1.6 %collective-permute-start.14 = (f32[2,128]{0,1:T(8,128)S(1)}, f32[2,128]{0,1:T(8,128)S(1)}, u32[]{:S(2)}, u32[]{:S(2)}) collective-permute-start(f32[2,128]{0,1:T(8,128)S(1)} %broadcast_in_dim.10), channel_id=1, source_target_pairs={{0,1},{1,0},{2,3},{3,2},{4,5},{5,4},{6,7},{7,6},{8,9},{9,8},{10,11... | collective-permute-start | bytes 3080 | tf_op jit(solution)/shard_map/ppermute | solution.py:331
  65.9 2.6 %collective-permute-done.14 = f32[2,128]{0,1:T(8,128)S(1)} collective-permute-done((f32[2,128]{0,1:T(8,128)S(1)}, f32[2,128]{0,1:T(8,128)S(1)}, u32[]{:S(2)}, u32[]{:S(2)}) %collective-permute-start.14) | collective-permute-done | bytes 1056 | tf_op jit(solution)/shard_map/ppermute | solution.py:331
  68.7 4.3 %collective-permute-done.15 = f32[2,128]{0,1:T(8,128)S(1)} collective-permute-done((f32[2,128]{0,1:T(8,128)S(1)}, f32[2,128]{0,1:T(8,128)S(1)}, u32[]{:S(2)}, u32[]{:S(2)}) %collective-permute-start.15) | collective-permute-done | bytes 1056 | tf_op jit(solution)/shard_map/ppermute | solution.py:331
  73.1 0.7 maximum_bitcast_fusion
  73.7 4.6 %collective-permute-done.16 = f32[2,128]{0,1:T(8,128)S(1)} collective-permute-done((f32[2,128]{0,1:T(8,128)S(1)}, f32[2,128]{0,1:T(8,128)S(1)}, u32[]{:S(2)}, u32[]{:S(2)}) %collective-permute-start.16) | collective-permute-done | bytes 1056 | tf_op jit(solution)/shard_map/ppermute | solution.py:331
  (55 shorter events, 3.8 us)
Async XLA Ops:
  1.5 9.4 %collective-permute-start.4 = (bf16[2,64,128]{2,1,0:T(8,128)(2,1)S(1)}, bf16[2,64,128]{2,1,0:T(8,128)(2,1)S(1)}, u32[]{:S(2)}, u32[]{:S(2)}) collective-permute-start(bf16[2,64,128]{2,1,0:T(8,128)(2,1)S(1)} %convert_bitcast_fusion), channel_id=1, source_target_pairs={{0,14},{1,15},{2,8},{3,9},{4,10},{5,11},{6,12},{7,13},{8,22},{9,23... | collective-permute-start | bytes 98312 | tf_op jit(solution)/shard_map/ppermute | solution.py:314
  6.0 8.6 %collective-permute-start.3 = (bf16[2,64,128]{2,1,0:T(8,128)(2,1)S(1)}, bf16[2,64,128]{2,1,0:T(8,128)(2,1)S(1)}, u32[]{:S(2)}, u32[]{:S(2)}) collective-permute-start(bf16[2,64,128]{2,1,0:T(8,128)(2,1)S(1)} %convert_bitcast_fusion), channel_id=1, source_target_pairs={{0,15},{1,8},{2,9},{3,10},{4,11},{5,12},{6,13},{7,14},{8,23},{9,16... | collective-permute-start | bytes 98312 | tf_op jit(solution)/shard_map/ppermute | solution.py:314
  8.6 6.6 %collective-permute-start.2 = (bf16[2,64,128]{2,1,0:T(8,128)(2,1)S(1)}, bf16[2,64,128]{2,1,0:T(8,128)(2,1)S(1)}, u32[]{:S(2)}, u32[]{:S(2)}) collective-permute-start(bf16[2,64,128]{2,1,0:T(8,128)(2,1)S(1)} %convert_bitcast_fusion), channel_id=1, source_target_pairs={{0,8},{1,9},{2,10},{3,11},{4,12},{5,13},{6,14},{7,15},{8,16},{9,17... | collective-permute-start | bytes 98312 | tf_op jit(solution)/shard_map/ppermute | solution.py:314
  8.6 8.0 %collective-permute-start.1 = (bf16[2,64,128]{2,1,0:T(8,128)(2,1)S(1)}, bf16[2,64,128]{2,1,0:T(8,128)(2,1)S(1)}, u32[]{:S(2)}, u32[]{:S(2)}) collective-permute-start(bf16[2,64,128]{2,1,0:T(8,128)(2,1)S(1)} %convert_bitcast_fusion), channel_id=1, source_target_pairs={{0,9},{1,10},{2,11},{3,12},{4,13},{5,14},{6,15},{7,8},{8,17},{9,18... | collective-permute-start | bytes 98312 | tf_op jit(solution)/shard_map/ppermute | solution.py:314
  10.4 12.5 %collective-permute-start.8 = (bf16[2,2,64,128]{3,2,1,0:T(8,128)(2,1)S(1)}, bf16[2,2,64,128]{3,2,1,0:T(8,128)(2,1)S(1)}, u32[]{:S(2)}, u32[]{:S(2)}) collective-permute-start(bf16[2,2,64,128]{3,2,1,0:T(8,128)(2,1)S(1)} %bitcast_convert_fusion), channel_id=1, source_target_pairs={{0,6},{1,7},{2,0},{3,1},{4,2},{5,3},{6,4},{7,5},{8,14},{9,15},{10,... | collective-permute-start | bytes 196616 | tf_op jit(solution)/shard_map/ppermute | solution.py:314
  10.9 8.7 %copy-start.6 = (bf16[2,64,128]{2,1,0:T(8,128)(2,1)}, bf16[2,64,128]{2,1,0:T(8,128)(2,1)S(1)}, u32[]{:S(2)}) copy-start(bf16[2,64,128]{2,1,0:T(8,128)(2,1)S(1)} %collective-permute-done.4.refs_4_) | copy-start | bytes 98308
  10.9 12.0 %collective-permute-start.7 = (bf16[2,2,64,128]{3,2,1,0:T(8,128)(2,1)S(1)}, bf16[2,2,64,128]{3,2,1,0:T(8,128)(2,1)S(1)}, u32[]{:S(2)}, u32[]{:S(2)}) collective-permute-start(bf16[2,2,64,128]{3,2,1,0:T(8,128)(2,1)S(1)} %bitcast_convert_fusion), channel_id=1, source_target_pairs={{0,7},{1,0},{2,1},{3,2},{4,3},{5,4},{6,5},{7,6},{8,15},{9,8},{10,9... | collective-permute-start | bytes 196616 | tf_op jit(solution)/shard_map/ppermute | solution.py:314
  14.6 5.0 %copy-start.7 = (bf16[2,64,128]{2,1,0:T(8,128)(2,1)}, bf16[2,64,128]{2,1,0:T(8,128)(2,1)S(1)}, u32[]{:S(2)}) copy-start(bf16[2,64,128]{2,1,0:T(8,128)(2,1)S(1)} %collective-permute-done.3.refs_3_) | copy-start | bytes 98308
  14.6 8.3 %collective-permute-start.6 = (bf16[2,2,64,128]{3,2,1,0:T(8,128)(2,1)S(1)}, bf16[2,2,64,128]{3,2,1,0:T(8,128)(2,1)S(1)}, u32[]{:S(2)}, u32[]{:S(2)}) collective-permute-start(bf16[2,2,64,128]{3,2,1,0:T(8,128)(2,1)S(1)} %bitcast_convert_fusion), channel_id=1, source_target_pairs={{0,1},{1,2},{2,3},{3,4},{4,5},{5,6},{6,7},{7,0},{8,9},{9,10},{10,1... | collective-permute-start | bytes 196616 | tf_op jit(solution)/shard_map/ppermute | solution.py:314
  15.2 4.4 %copy-start.8 = (bf16[2,64,128]{2,1,0:T(8,128)(2,1)}, bf16[2,64,128]{2,1,0:T(8,128)(2,1)S(1)}, u32[]{:S(2)}) copy-start(bf16[2,64,128]{2,1,0:T(8,128)(2,1)S(1)} %collective-permute-done.2.refs_2_) | copy-start | bytes 98308
  15.2 7.8 %collective-permute-start.5 = (bf16[2,2,64,128]{3,2,1,0:T(8,128)(2,1)S(1)}, bf16[2,2,64,128]{3,2,1,0:T(8,128)(2,1)S(1)}, u32[]{:S(2)}, u32[]{:S(2)}) collective-permute-start(bf16[2,2,64,128]{3,2,1,0:T(8,128)(2,1)S(1)} %bitcast_convert_fusion), channel_id=1, source_target_pairs={{0,2},{1,3},{2,4},{3,5},{4,6},{5,7},{6,0},{7,1},{8,10},{9,11},{10,... | collective-permute-start | bytes 196616 | tf_op jit(solution)/shard_map/ppermute | solution.py:314
  16.6 6.3 %collective-permute-start = (bf16[2,64,128]{2,1,0:T(8,128)(2,1)S(1)}, bf16[2,64,128]{2,1,0:T(8,128)(2,1)S(1)}, u32[]{:S(2)}, u32[]{:S(2)}) collective-permute-start(bf16[2,64,128]{2,1,0:T(8,128)(2,1)S(1)} %convert_bitcast_fusion), channel_id=1, source_target_pairs={{0,10},{1,11},{2,12},{3,13},{4,14},{5,15},{6,8},{7,9},{8,18},{9,19... | collective-permute-start | bytes 98312 | tf_op jit(solution)/shard_map/ppermute | solution.py:314
  36.3 6.9 %collective-permute-start.13 = (bf16[2,64,128]{2,1,0:T(8,128)(2,1)}, bf16[2,64,128]{2,1,0:T(8,128)(2,1)S(1)}, u32[]{:S(2)}, u32[]{:S(2)}) collective-permute-start(bf16[2,64,128]{2,1,0:T(8,128)(2,1)} %get-tuple-element.22), channel_id=1, source_target_pairs={{0,14},{1,15},{2,8},{3,9},{4,10},{5,11},{6,12},{7,13},{8,22},{9,23... | collective-permute-start | bytes 98312 | tf_op jit(solution)/shard_map/ppermute | solution.py:314
  37.5 5.7 %collective-permute-start.12 = (bf16[2,64,128]{2,1,0:T(8,128)(2,1)}, bf16[2,64,128]{2,1,0:T(8,128)(2,1)S(1)}, u32[]{:S(2)}, u32[]{:S(2)}) collective-permute-start(bf16[2,64,128]{2,1,0:T(8,128)(2,1)} %get-tuple-element.22), channel_id=1, source_target_pairs={{0,15},{1,8},{2,9},{3,10},{4,11},{5,12},{6,13},{7,14},{8,23},{9,16... | collective-permute-start | bytes 98312 | tf_op jit(solution)/shard_map/ppermute | solution.py:314
  39.7 3.7 %collective-permute-start.11 = (bf16[2,64,128]{2,1,0:T(8,128)(2,1)}, bf16[2,64,128]{2,1,0:T(8,128)(2,1)S(1)}, u32[]{:S(2)}, u32[]{:S(2)}) collective-permute-start(bf16[2,64,128]{2,1,0:T(8,128)(2,1)} %get-tuple-element.22), channel_id=1, source_target_pairs={{0,8},{1,9},{2,10},{3,11},{4,12},{5,13},{6,14},{7,15},{8,16},{9,17... | collective-permute-start | bytes 98312 | tf_op jit(solution)/shard_map/ppermute | solution.py:314
  40.4 7.3 %collective-permute-start.10 = (bf16[2,64,128]{2,1,0:T(8,128)(2,1)}, bf16[2,64,128]{2,1,0:T(8,128)(2,1)S(1)}, u32[]{:S(2)}, u32[]{:S(2)}) collective-permute-start(bf16[2,64,128]{2,1,0:T(8,128)(2,1)} %get-tuple-element.22), channel_id=1, source_target_pairs={{0,9},{1,10},{2,11},{3,12},{4,13},{5,14},{6,15},{7,8},{8,17},{9,18... | collective-permute-start | bytes 98312 | tf_op jit(solution)/shard_map/ppermute | solution.py:314
  40.5 7.3 %collective-permute-start.9 = (bf16[2,64,128]{2,1,0:T(8,128)(2,1)}, bf16[2,64,128]{2,1,0:T(8,128)(2,1)S(1)}, u32[]{:S(2)}, u32[]{:S(2)}) collective-permute-start(bf16[2,64,128]{2,1,0:T(8,128)(2,1)} %get-tuple-element.22), channel_id=1, source_target_pairs={{0,10},{1,11},{2,12},{3,13},{4,14},{5,15},{6,8},{7,9},{8,18},{9,19... | collective-permute-start | bytes 98312 | tf_op jit(solution)/shard_map/ppermute | solution.py:314
  43.3 4.4 %copy-start.10 = (bf16[2,64,128]{2,1,0:T(8,128)(2,1)}, bf16[2,64,128]{2,1,0:T(8,128)(2,1)S(1)}, u32[]{:S(2)}) copy-start(bf16[2,64,128]{2,1,0:T(8,128)(2,1)S(1)} %collective-permute-done.13.refs_4_) | copy-start | bytes 98308
  43.3 4.4 %copy-start.11 = (bf16[2,64,128]{2,1,0:T(8,128)(2,1)}, bf16[2,64,128]{2,1,0:T(8,128)(2,1)S(1)}, u32[]{:S(2)}) copy-start(bf16[2,64,128]{2,1,0:T(8,128)(2,1)S(1)} %collective-permute-done.12.refs_3_) | copy-start | bytes 98308
  64.3 4.3 %collective-permute-start.14 = (f32[2,128]{0,1:T(8,128)S(1)}, f32[2,128]{0,1:T(8,128)S(1)}, u32[]{:S(2)}, u32[]{:S(2)}) collective-permute-start(f32[2,128]{0,1:T(8,128)S(1)} %broadcast_in_dim.10), channel_id=1, source_target_pairs={{0,1},{1,0},{2,3},{3,2},{4,5},{5,4},{6,7},{7,6},{8,9},{9,8},{10,11... | collective-permute-start | bytes 3080 | tf_op jit(solution)/shard_map/ppermute | solution.py:331
  68.6 4.4 %copy-start.4 = (f32[2,64,128]{2,1,0:T(8,128)S(1)}, f32[2,64,128]{2,1,0:T(8,128)}, u32[]{:S(2)}) copy-start(f32[2,64,128]{2,1,0:T(8,128)} %get-tuple-element.21) | copy-start | bytes 196612
  68.6 4.4 %copy-start.5 = (f32[2,64,128]{2,1,0:T(8,128)S(1)}, f32[2,64,128]{2,1,0:T(8,128)}, u32[]{:S(2)}) copy-start(f32[2,64,128]{2,1,0:T(8,128)} %get-tuple-element.23) | copy-start | bytes 196612
  68.6 4.3 %collective-permute-start.15 = (f32[2,128]{0,1:T(8,128)S(1)}, f32[2,128]{0,1:T(8,128)S(1)}, u32[]{:S(2)}, u32[]{:S(2)}) collective-permute-start(f32[2,128]{0,1:T(8,128)S(1)} %broadcast_add_fusion), channel_id=1, source_target_pairs={{0,2},{1,3},{2,0},{3,1},{4,6},{5,7},{6,4},{7,5},{8,10},{9,11},{10,... | collective-permute-start | bytes 3080 | tf_op jit(solution)/shard_map/ppermute | solution.py:331
  73.0 5.4 %collective-permute-start.16 = (f32[2,128]{0,1:T(8,128)S(1)}, f32[2,128]{0,1:T(8,128)S(1)}, u32[]{:S(2)}, u32[]{:S(2)}) collective-permute-start(f32[2,128]{0,1:T(8,128)S(1)} %fusion.1), channel_id=1, source_target_pairs={{0,4},{1,5},{2,6},{3,7},{4,0},{5,1},{6,2},{7,3},{8,12},{9,13},{10,... | collective-permute-start | bytes 3080 | tf_op jit(solution)/shard_map/ppermute | solution.py:331
  (9 other events, 11.7 us)
